TPU v7x, 512 devices: a whole 4x8x8 slice. The times are simulated.
512 devices in a mesh: row: 16 (over y, core), col: 32 (over z, x).
Axes of the slice: x: 4, y: 8, z: 8, core: 2. Of those that a mesh axis runs over, the one named last changes fastest.
Arguments:
- features: bfloat16 [65536, 128], P(('row', 'col')), may hold values from -6 to 6
- block_values: bfloat16 [16, 32, 128, 128, 128], P('row', 'col'), may hold values from -0.046875 to 0.046875
- block_rows: int32 [16, 32, 128], P('row', 'col'), may hold values from 0 to 31
- block_cols: int32 [16, 32, 128], P('row', 'col'), may hold values from 0 to 15
- counts: int32 [16, 32], P('row', 'col'), may hold values from 16 to 128, as said below
- weight: float32 [128, 128], replicated, may hold values from -0.5 to 0.5
- bias: float32 [128], replicated, may hold values from -3 to 3
- cotangent: bfloat16 [65536, 128], P(('row', 'col')), may hold values from -6 to 6
Outputs:
- hidden: float32 [65536, 128], P(('row', 'col'))
- grad_features: float32 [65536, 128], P(('row', 'col'))
- grad_weight: float32 [128, 128], replicated
- grad_bias: float32 [128], replicated
Inputs may be any that keep to these rules, and one draw needn't show every extreme that they name: `counts`: some tile has all 128 slots live.
All inputs are finite; a program needn't handle non-finite values.
Results may differ from a plain program's by a relative error of at most 0.0029.
Values may be sent and summed in bfloat16 or wider, within the bound.
A program may use at most 128 MiB of HBM per device.

v0:
```python
import math

import jax
import jax.numpy as jnp
from jax import lax
from jax.sharding import PartitionSpec as P


def tile_product(tile_values, out_index, in_index, live_count, source, out_blocks, transposed):
    slot_count = tile_values.shape[0]
    block_size = tile_values.shape[1]
    feat_width = source.shape[1]
    source_blocks = source.reshape(-1, block_size, feat_width)
    picked = source_blocks[in_index]
    if transposed:
        products = jnp.einsum(
            "kab,kaf->kbf", tile_values, picked, preferred_element_type=jnp.float32
        )
    else:
        products = jnp.einsum(
            "kab,kbf->kaf", tile_values, picked, preferred_element_type=jnp.float32
        )
    block_ids = jnp.arange(out_blocks, dtype=jnp.int32)
    slot_ids = jnp.arange(slot_count, dtype=jnp.int32)
    live_mask = slot_ids < live_count
    onehot = ((out_index[None, :] == block_ids[:, None]) & live_mask[None, :]).astype(jnp.float32)
    totals = jnp.dot(
        onehot, products.reshape(slot_count, block_size * feat_width), precision=lax.Precision.HIGH
    )
    return totals.reshape(out_blocks * block_size, feat_width)


def activate(pre_act, cotangent):
    sigm = 1.0 / (1.0 + jnp.exp(-pre_act))
    hidden = pre_act * sigm
    masked_grad = cotangent.astype(jnp.float32) * sigm * (1.0 + pre_act * (1.0 - sigm))
    return (hidden, masked_grad)


def per_device(features, block_values, block_rows, block_cols, counts, weight, bias, cotangent):
    block_size = features.shape[0]
    row_count = lax.axis_size("row")
    col_count = lax.axis_size("col")
    tile_values = block_values[0, 0]
    tile_rows = block_rows[0, 0]
    tile_cols = block_cols[0, 0]
    live_count = counts[0, 0]
    column_feats = lax.all_gather(features, "row", axis=0, tiled=True)
    partial_value = tile_product(
        tile_values, tile_rows, tile_cols, live_count, column_feats, col_count, False
    )
    agg_own = lax.psum_scatter(partial_value, "col", scatter_dimension=0, tiled=True)
    pre_act = jnp.dot(agg_own, weight, precision=lax.Precision.HIGHEST) + bias[None, :]
    hidden, masked_grad = activate(pre_act, cotangent)
    grad_own = jnp.dot(masked_grad, weight.T, precision=lax.Precision.HIGHEST).astype(jnp.bfloat16)
    grad_row = lax.all_gather(grad_own, "col", axis=0, tiled=True)
    back_partial = tile_product(
        tile_values, tile_cols, tile_rows, live_count, grad_row, row_count, True
    )
    grad_features = lax.psum_scatter(back_partial, "row", scatter_dimension=0, tiled=True)
    norm_factor = 1.0 / math.sqrt(block_size * row_count * col_count)
    weight_part = jnp.dot(agg_own.T, masked_grad, precision=lax.Precision.HIGHEST) * norm_factor
    bias_part = jnp.sum(masked_grad, axis=0) * norm_factor
    grad_weight, grad_bias = lax.psum((weight_part, bias_part), ("row", "col"))
    return (hidden, grad_features, grad_weight, grad_bias)


def solution(mesh):
    placed = (
        P(("row", "col"), None),
        P("row", "col", None, None, None),
        P("row", "col", None),
        P("row", "col", None),
        P("row", "col"),
        P(),
        P(),
        P(("row", "col"), None),
    )
    return jax.shard_map(
        per_device,
        mesh=mesh,
        in_specs=placed,
        out_specs=(P(("row", "col"), None), P(("row", "col"), None), P(), P()),
        check_vma=False,
    )
```

profile of v0, /device:TPU:1, one launch (start us, length us, event | category | flops | bytes accessed | tf_op | source)
XLA Modules:
  0.0 697.8 jit_solution(4192147037128711479)
XLA Ops:
  7.9 0.7 fusion.21
  8.6 22.6 %all_gather.6 = bf16[2048,128]{1,0:T(8,128)(2,1)S(1)} all-gather(bf16[128,128]{1,0:T(8,128)(2,1)} %param.8), channel_id=1, replica_groups=mesh['row'=16,'col'=32] {'row'}, dimensions={0}, use_global_device_ids=true | all-gather | bytes 557056 | tf_op jit(solution)/shard_map/all_gather | solution.py:48
  31.2 3.0 gather_fusion
  34.2 9.8 %fusion.4 = f32[128,128,128]{1,2,0:T(8,128)} fusion(bf16[128,128,128]{2,1,0:T(8,128)(2,1)} %gather_fusion, bf16[1,1,128,128,128]{4,3,2,1,0:T(8,128)(2,1)} %param.9), kind=kOutput, calls=%fused_computation.6 | convolution fusion | flops 536870912 | bytes 16777216 | tf_op jit(solution)/shard_map/kab,kbf->kaf/dot_general | solution.py:20
  44.0 9.3 %copy.13 = f32[128,128,128]{0,2,1:T(8,128)} copy(f32[128,128,128]{1,2,0:T(8,128)} %fusion.4) | data formatting | bytes 16777216 | tf_op jit(solution)/shard_map/kab,kbf->kaf/dot_general | solution.py:20
  53.3 6.2 fusion.12
  59.5 1.5 reshape.91
  61.1 0.0 all-gather.2.cloned.1.call-start
  61.1 218.9 %reduce-scatter.3.cloned.1.call-done = f32[128,128]{1,0:T(8,128)} async-done(((f32[4096,128]{1,0:T(8,128)}), f32[128,128]{1,0:T(8,128)}) %reduce-scatter.3.cloned.1.call-update) | async-done | bytes 65552 | tf_op jit(solution)/shard_map/reduce_scatter | solution.py:52
  280.1 1.7 fusion.23
  281.8 0.9 convolution_convert_fusion
  282.7 0.0 all-reduce.2.cloned.1.call-start
  282.7 1.8 convolution_multiply_fusion
  284.5 0.2 reduce-scatter.5.cloned.1.call-start
  284.8 79.4 %all-gather.2.cloned.1.call-done = bf16[4096,128]{1,0:T(8,128)(2,1)} async-done(((bf16[128,128]{1,0:T(8,128)(2,1)}), bf16[4096,128]{1,0:T(8,128)(2,1)}) %all-gather.2.cloned.1.call-update) | async-done | bytes 1048592 | tf_op jit(solution)/shard_map/all_gather | solution.py:56
  364.1 4.3 gather_fusion.1
  368.4 8.2 %fusion.7 = f32[128,128,128]{1,2,0:T(8,128)} fusion(bf16[128,128,128]{2,1,0:T(8,128)(2,1)} %gather_fusion.1, bf16[1,1,128,128,128]{4,3,2,1,0:T(8,128)(2,1)} %param.9), kind=kOutput, calls=%fused_computation.7 | convolution fusion | flops 536870912 | bytes 16777216 | tf_op jit(solution)/shard_map/kab,kaf->kbf/dot_general | solution.py:16
  376.6 9.3 %copy.15 = f32[128,128,128]{0,2,1:T(8,128)} copy(f32[128,128,128]{1,2,0:T(8,128)} %fusion.7) | data formatting | bytes 16777216 | tf_op jit(solution)/shard_map/kab,kaf->kbf/dot_general | solution.py:16
  385.9 5.7 fusion.16
  391.6 1.1 reshape.94
  392.8 101.6 %psum.15 = f32[128]{0:T(128)} all-reduce(f32[128]{0:T(128)S(1)} %broadcast_multiply_fusion), channel_id=1, replica_groups=mesh['row'=16,'col'=32] {'row','col'}, use_global_device_ids=true, to_apply=%region_4.0 | all-reduce | flops 128 | bytes 1024 | tf_op jit(solution)/shard_map/psum | solution.py:64
  494.4 141.8 %all-reduce.2.cloned.1.call-done = f32[128,128]{1,0:T(8,128)} async-done(((f32[128,128]{1,0:T(8,128)}), f32[128,128]{1,0:T(8,128)}) %all-reduce.2.cloned.1.call-update) | async-done | bytes 65552 | tf_op jit(solution)/shard_map/psum | solution.py:64
  636.2 53.6 %reduce-scatter.5.cloned.1.call-done = f32[128,128]{1,0:T(8,128)} async-done(((f32[2048,128]{1,0:T(8,128)}), f32[128,128]{1,0:T(8,128)}) %reduce-scatter.5.cloned.1.call-update) | async-done | bytes 65552 | tf_op jit(solution)/shard_map/reduce_scatter | solution.py:60
  689.8 1.5 copy.20
  (20 shorter events, 0.2 us)
Async XLA Ops:
  7.2 272.9 %copy-start = (f32[128,128]{1,0:T(8,128)S(1)}, f32[128,128]{1,0:T(8,128)}, u32[]{:S(2)}) copy-start(f32[128,128]{1,0:T(8,128)} %param.13) | copy-start | bytes 196612
  7.2 272.9 %reduce-scatter.3.cloned.1.call-start = ((), (), s32[]{:S(2)}) async-start(), calls=%async_computation.2 | async-start | bytes 2162688 | tf_op jit(solution)/shard_map/reduce_scatter | solution.py:52
  44.0 9.3 %copy-start.1 = (s32[1,1,128]{2,1,0:T(1,128)S(1)}, s32[1,1,128]{2,1,0:T(1,128)}, u32[]{:S(2)}) copy-start(s32[1,1,128]{2,1,0:T(1,128)} %param.10) | copy-start | bytes 1540
  59.5 220.6 %copy-start.3 = (bf16[128,128]{1,0:T(8,128)(2,1)S(1)}, bf16[128,128]{1,0:T(8,128)(2,1)}, u32[]{:S(2)}) copy-start(bf16[128,128]{1,0:T(8,128)(2,1)} %param.15) | copy-start | bytes 98308
  59.5 220.5 %copy-start.4 = (f32[128]{0:T(128)S(1)}, f32[128]{0:T(128)}, u32[]{:S(2)}) copy-start(f32[128]{0:T(128)} %param.14) | copy-start | bytes 1540
  61.1 303.1 %all-gather.2.cloned.1.call-start = ((), (), s32[]{:S(2)}) async-start(), calls=%async_computation.3 | async-start | bytes 1081344 | tf_op jit(solution)/shard_map/all_gather | solution.py:56
  282.7 353.5 %all-reduce.2.cloned.1.call-start = ((), (), s32[]{:S(2)}) async-start(), calls=%async_computation.5 | async-start | bytes 131072 | tf_op jit(solution)/shard_map/psum | solution.py:64
  284.5 405.3 %reduce-scatter.5.cloned.1.call-start = ((), (), s32[]{:S(2)}) async-start(), calls=%async_computation.4 | async-start | bytes 1114112 | tf_op jit(solution)/shard_map/reduce_scatter | solution.py:60
  376.6 9.3 %copy-start.2 = (s32[1,1,128]{2,1,0:T(1,128)S(1)}, s32[1,1,128]{2,1,0:T(1,128)}, u32[]{:S(2)}) copy-start(s32[1,1,128]{2,1,0:T(1,128)} %param.11) | copy-start | bytes 1540
Sparse Core Ops, SparseCore 0:
  61.2 218.8 reduce-scatter.2
  283.8 80.2 all-gather.1
  369.7 266.4 all-reduce.1
  639.4 50.3 reduce-scatter.4
where the time goes:
time: 700 us; the launch traced here: 698 us
  waiting for transfers between devices  494 us (71%)
  blocking collectives  124 us (18%)
  matrix products  34.2 us (5%)
  local copies, waits for them, and re-layouts  30.1 us (4%)
  between operations  14.5 us (2%)
    reduce_scatter x1, waiting for transfers between devices, per_device(): lax.psum_scatter(partial_value, 'col', scatter_dimension=0, tiled=True)  219 us
    psum x1, waiting for transfers between devices, per_device(): grad_weight, grad_bias = lax.psum((weight_part, bias_part), ('row', 'col'))  142 us
    psum x1, blocking collectives, per_device(): grad_weight, grad_bias = lax.psum((weight_part, bias_part), ('row', 'col'))  102 us
    all_gather x1, waiting for transfers between devices, per_device(): grad_row = lax.all_gather(grad_own, 'col', axis=0, tiled=True)  79.4 us
    reduce_scatter x1, waiting for transfers between devices, per_device(): lax.psum_scatter(back_partial, 'row', scatter_dimension=0, tiled=True)  53.6 us
    all_gather x1, blocking collectives, per_device(): column_feats = lax.all_gather(features, 'row', axis=0, tiled=True)  22.6 us
  transfers between devices with their start and end apart: 4, of which 4 were waited for; matrix products, arithmetic and copies ran while one was open for 4% of the time, Pallas kernels for 0%

commit v1 on v0

v1 whole, which is shorter than its diff:
```python
import functools
import math

import jax
import jax.numpy as jnp
from jax import lax
from jax.experimental import pallas as pl
from jax.experimental.pallas import tpu as pltpu
from jax.sharding import PartitionSpec as P

MESH = pl.DeviceIdType.MESH
CHUNK = 16


def product_kernel(transposed, out_blocks, dest_ref, from_ref, count_ref, values_ref, source_ref, out_ref, totals):
    step = pl.program_id(0)
    live = count_ref[0]

    @pl.when(step == 0)
    def _():
        totals[...] = jnp.zeros_like(totals)

    @pl.when(step * CHUNK < live)
    def _():
        for k in range(CHUNK):
            slot = step * CHUNK + k
            dest = jnp.where(slot < live, dest_ref[slot], out_blocks)
            block = values_ref[k]
            source = source_ref[from_ref[slot]]
            if transposed:
                part = jnp.dot(source, block, preferred_element_type=jnp.float32)
            else:
                part = jnp.dot(block, source, preferred_element_type=jnp.float32)
            totals[dest] += part

    @pl.when(step == pl.num_programs(0) - 1)
    def _():
        out_ref[...] = totals[0:out_blocks].astype(out_ref.dtype)


def tile_product(values, dest, source_of, count, source, out_blocks, transposed, out_dtype):
    slots, size, _ = values.shape
    width = source.shape[2]
    return pl.pallas_call(
        functools.partial(product_kernel, transposed, out_blocks),
        grid_spec=pltpu.PrefetchScalarGridSpec(
            num_scalar_prefetch=3,
            grid=(slots // CHUNK,),
            in_specs=[
                pl.BlockSpec((CHUNK, size, size), lambda i, *_: (i, 0, 0)),
                pl.BlockSpec(source.shape, lambda i, *_: (0, 0, 0)),
            ],
            out_specs=pl.BlockSpec((out_blocks, size, width), lambda i, *_: (0, 0, 0)),
            scratch_shapes=[pltpu.VMEM((out_blocks + 1, size, width), jnp.float32)],
        ),
        out_shape=jax.ShapeDtypeStruct((out_blocks, size, width), out_dtype),
        compiler_params=pltpu.CompilerParams(dimension_semantics=("arbitrary",)),
    )(dest, source_of, count, values, source)


def exchange_kernel(axis, n, kinds, *refs):
    m = len(kinds)
    sources, outs, held = refs[:m], refs[m : 2 * m], refs[2 * m : 3 * m]
    send_sem, recv_sem = refs[3 * m], refs[3 * m + 1]
    me = lax.axis_index(axis)
    row, col = lax.axis_index("row"), lax.axis_index("col")

    def device(peer):
        return (row, peer) if axis == "col" else (peer, col)

    def partner(k):
        half = k // 2 + 1
        return lax.rem(me + jnp.where(k % 2 == 0, half, n - half), n)

    def copy(i, to, slot):
        source = sources[i].at[to] if kinds[i] == "scatter" else sources[i]
        return pltpu.make_async_remote_copy(
            src_ref=source,
            dst_ref=held[i].at[slot],
            send_sem=send_sem.at[i, to],
            recv_sem=recv_sem.at[i, slot],
            device_id=device(to),
            device_id_type=MESH,
        )

    barrier = pltpu.get_barrier_semaphore()

    @pl.loop(0, n - 1)
    def _(k):
        pl.semaphore_signal(barrier, inc=1, device_id=device(partner(k)), device_id_type=MESH)

    pl.semaphore_wait(barrier, n - 1)

    @pl.loop(0, n - 1)
    def _(k):
        for i in range(m):
            copy(i, partner(k), me).start()

    for i in range(m):
        held[i][me] = sources[i][me] if kinds[i] == "scatter" else sources[i][...]

    @pl.loop(0, n - 1)
    def _(k):
        for i in range(m):
            copy(i, partner(k), partner(k)).wait_recv()

    for i in range(m):
        if kinds[i] == "gather":
            outs[i][...] = held[i][...]
        else:

            def add(s, total):
                return total + held[i][s].astype(jnp.float32)

            outs[i][...] = lax.fori_loop(0, n, add, jnp.zeros(outs[i].shape, jnp.float32))

    @pl.loop(0, n - 1)
    def _(k):
        for i in range(m):
            copy(i, partner(k), partner(k)).wait_send()


def exchange(axis, number, *items):
    n = lax.axis_size(axis)
    kinds = tuple(kind for kind, _ in items)
    arrays = [array for _, array in items]
    blocks = [a.shape[1:] if kind == "scatter" else a.shape for kind, a in items]
    vmem = pl.BlockSpec(memory_space=pltpu.VMEM)
    return pl.pallas_call(
        functools.partial(exchange_kernel, axis, n, kinds),
        out_shape=[
            jax.ShapeDtypeStruct((n,) + block, a.dtype) if kind == "gather" else jax.ShapeDtypeStruct(block, jnp.float32)
            for (kind, a), block in zip(items, blocks)
        ],
        in_specs=[vmem] * len(items),
        out_specs=[vmem] * len(items),
        scratch_shapes=[pltpu.VMEM((n,) + block, a.dtype) for a, block in zip(arrays, blocks)]
        + [pltpu.SemaphoreType.DMA((len(items), n)), pltpu.SemaphoreType.DMA((len(items), n))],
        compiler_params=pltpu.CompilerParams(collective_id=number, has_side_effects=True),
    )(*arrays)


def per_device(features, block_values, block_rows, block_cols, counts, weight, bias, cotangent):
    size, width = features.shape
    hidden_width = weight.shape[1]
    row_count = lax.axis_size("row")
    col_count = lax.axis_size("col")
    values = block_values[0, 0]
    rows = block_rows[0, 0]
    cols = block_cols[0, 0]
    count = counts[0]

    (column_feats,) = exchange("row", 0, ("gather", features))
    partial = tile_product(values, rows, cols, count, column_feats, col_count, False, jnp.bfloat16)
    (aggregated,) = exchange("col", 1, ("scatter", partial))

    highest = lax.Precision.HIGHEST
    pre_act = jnp.dot(aggregated, weight, precision=highest) + bias[None, :]
    sigm = 1.0 / (1.0 + jnp.exp(-pre_act))
    hidden = pre_act * sigm
    masked_grad = cotangent.astype(jnp.float32) * sigm * (1.0 + pre_act * (1.0 - sigm))
    grad_own = lax.dot_general(
        weight, masked_grad, (((1,), (1,)), ((), ())), precision=highest
    ).astype(jnp.bfloat16)
    norm_factor = 1.0 / math.sqrt(size * row_count * col_count)
    weight_part = jnp.dot(aggregated.T, masked_grad, precision=highest) * norm_factor
    bias_part = jnp.sum(masked_grad, axis=0) * norm_factor
    per_slice = width // col_count
    slices = jnp.concatenate(
        [
            weight_part.reshape(col_count, per_slice, hidden_width),
            jnp.broadcast_to(bias_part, (col_count, 1, hidden_width)),
            jnp.zeros((col_count, -(per_slice + 1) % 8, hidden_width), jnp.float32),
        ],
        axis=1,
    )

    grad_row, col_slice = exchange("col", 2, ("gather", grad_own), ("scatter", slices))
    back = tile_product(values, cols, rows, count, grad_row, row_count, True, jnp.bfloat16)
    grad_t, own_slice = exchange("row", 3, ("scatter", back), ("collect", col_slice))
    (all_slices,) = exchange("col", 4, ("gather", own_slice))
    grad_weight = all_slices[:, :per_slice].reshape(width, hidden_width)
    grad_bias = all_slices[0, per_slice]
    return (hidden, grad_t.T, grad_weight, grad_bias)


def solution(mesh):
    placed = (
        P(("row", "col"), None),
        P("row", "col", None, None, None),
        P("row", "col", None),
        P("row", "col", None),
        P("row", "col"),
        P(),
        P(),
        P(("row", "col"), None),
    )
    return jax.shard_map(
        per_device,
        mesh=mesh,
        in_specs=placed,
        out_specs=(P(("row", "col"), None), P(("row", "col"), None), P(), P()),
        check_vma=False,
    )
```

time: 700 us -> 162 us (0.23)
  waiting for transfers between devices: 494 us -> 0 us
  Pallas kernels: 0 us -> 150 us
  blocking collectives: 124 us -> 0 us
  matrix products: 34.2 us -> 3.71 us
  local copies, waits for them, and re-layouts: 30.1 us -> 4.4 us
  between operations: 14.5 us -> 1.44 us
    reduce_scatter x2 -> x0, waiting for transfers between devices: 273 us -> none  [the longest x1 219 us: per_device(): lax.psum_scatter(partial_value, 'col', scatter_dimension=0, tiled=True)]
    pallas_call x0 -> x7, Pallas kernels: none -> 150 us  [the longest x5 135 us: exchange(): pl.pallas_call(functools.partial(exchange_kernel, axis, n, kinds), out_sh...]
    psum x1 -> x0, waiting for transfers between devices: 142 us -> none  [per_device(): grad_weight, grad_bias = lax.psum((weight_part, bias_part), ('row', 'col'))]
    psum x1 -> x0, blocking collectives: 102 us -> none  [per_device(): grad_weight, grad_bias = lax.psum((weight_part, bias_part), ('row', 'col'))]
    all_gather x1 -> x0, waiting for transfers between devices: 79.4 us -> none  [per_device(): grad_row = lax.all_gather(grad_own, 'col', axis=0, tiled=True)]
    dot_general x7 -> x3, matrix products: 34.2 us -> 3.71 us  [the longest x1 1.71 us: per_device(): pre_act = jnp.dot(aggregated, weight, precision=highest) + bias[None, :]]
    all_gather x1 -> x0, blocking collectives: 22.6 us -> none  [per_device(): column_feats = lax.all_gather(features, 'row', axis=0, tiled=True)]
    dot_general x2 -> x0, local copies, waits for them, and re-layouts: 18.7 us -> none  [the longest x1 9.34 us: tile_product(): jnp.einsum('kab,kaf->kbf', tile_values, picked, preferred_element_type=jn...]
  transfers between devices with their start and end apart: 4 -> 0, of which waited for: 4 -> 0; matrix products, arithmetic and copies ran while one was open for 4% -> 0% of each run, Pallas kernels for 0% -> 0%
where the time goes in v1:
time: 162 us; the launch traced here: 161 us
  Pallas kernels  150 us (93%)
  local copies, waits for them, and re-layouts  4.4 us (3%)
  matrix products  3.71 us (2%)
    pallas_call x5, Pallas kernels, exchange(): pl.pallas_call(functools.partial(exchange_kernel, axis, n, kinds), out_sh...  135 us
    pallas_call x2, Pallas kernels, tile_product(): pl.pallas_call(functools.partial(product_kernel, transposed, out_blocks),...  15.2 us

profile of v1, /device:TPU:1, one launch (start us, length us, event | category | flops | bytes accessed | tf_op | source)
XLA Modules:
  0.0 160.8 jit_solution(5152559623065329129)
XLA Ops:
  0.6 0.0 copy-start
  0.6 0.0 copy-start.1
  0.7 0.0 copy-start.2
  1.4 0.1 pad.2.clone
  1.4 25.0 %shard_map.111.source_ref = bf16[16,128,128]{2,1,0:T(8,128)(2,1)} custom-call(bf16[128,128]{1,0:T(8,128)(2,1)} %refs_0_.1), custom_call_target="tpu_custom_call" | custom-call | tf_op jit(solution)/shard_map/pallas_call | solution.py:129
  26.5 7.7 %shard_map.112.refs_0_ = bf16[32,128,128]{2,1,0:T(8,128)(2,1)} custom-call(s32[128]{0:T(128)} %bitcast.24, s32[128]{0:T(128)} %bitcast.26, s32[1]{0:T(128)} %bitcast.17.count_ref, bf16[128,128,128]{2,1,0:T(8,128)(2,1)} %bitcast.19, bf16[16,128,128]{2,1,0:T(8,128)(2,1)} %shard_map.111.source_ref), custom_call_target="tpu_custom_call" | custom-call | tf_op jit(solution)/shard_map/pallas_call | solution.py:44
  34.1 32.0 %shard_map.113 = f32[128,128]{1,0:T(8,128)} custom-call(bf16[32,128,128]{2,1,0:T(8,128)(2,1)} %shard_map.112.refs_0_), custom_call_target="tpu_custom_call" | custom-call | tf_op jit(solution)/shard_map/pallas_call | solution.py:129
  66.1 0.0 copy-done
  66.1 0.0 copy-done.1
  66.1 0.0 copy-done.2
  66.1 1.7 %fusion.2 = (f32[128]{0:T(128)S(1)}, f32[128,128]{1,0:T(8,128)S(1)}, f32[128,128]{1,0:T(8,128)}) fusion(bf16[128,128]{1,0:T(8,128)(2,1)S(1)} %copy-done.1, f32[128]{0:T(128)S(1)} %copy-done.2, f32[128,128]{1,0:T(8,128)} %shard_map.113, f32[128,128]{1,0:T(8,128)S(1)} %copy-done), kind=kOutput, calls=%fused_computation.10 | convolution fusion | flops 25362304 | bytes 295936 | tf_op jit(solution)/shard_map/dot_general | solution.py:158
  67.8 1.1 convolution_multiply_fusion
  69.0 0.9 fusion.refs_0_
  69.9 0.7 maximum_maximum_fusion.refs_1_
  70.6 35.3 %shard_map.114 = (bf16[32,128,128]{2,1,0:T(8,128)(2,1)}, f32[8,128]{1,0:T(8,128)}) custom-call(bf16[128,128]{1,0:T(8,128)(2,1)} %fusion.refs_0_, f32[32,8,128]{2,1,0:T(8,128)} %maximum_maximum_fusion.refs_1_), custom_call_target="tpu_custom_call" | custom-call | tf_op jit(solution)/shard_map/pallas_call | solution.py:129
  106.0 7.5 %shard_map.115.refs_0_ = bf16[16,128,128]{2,1,0:T(8,128)(2,1)} custom-call(s32[128]{0:T(128)} %bitcast.27, s32[128]{0:T(128)} %bitcast.25, s32[1]{0:T(128)} %bitcast.18.count_ref, bf16[128,128,128]{2,1,0:T(8,128)(2,1)} %bitcast.20, bf16[32,128,128]{2,1,0:T(8,128)(2,1)} %get-tuple-element.8.source_ref), custom_call_target="tpu_custom_call" | custom-call | tf_op jit(solution)/shard_map/pallas_call | solution.py:44
  113.5 27.4 %shard_map.116 = (f32[128,128]{1,0:T(8,128)}, f32[8,128]{1,0:T(8,128)}) custom-call(bf16[16,128,128]{2,1,0:T(8,128)(2,1)} %shard_map.115.refs_0_, f32[8,128]{1,0:T(8,128)} %get-tuple-element.9.refs_1_), custom_call_target="tpu_custom_call" | custom-call | tf_op jit(solution)/shard_map/pallas_call | solution.py:129
  140.9 1.6 copy.13
  142.5 15.5 %shard_map.117 = f32[32,8,128]{2,1,0:T(8,128)} custom-call(f32[8,128]{1,0:T(8,128)} %get-tuple-element.11.refs_0_), custom_call_target="tpu_custom_call" | custom-call | tf_op jit(solution)/shard_map/pallas_call | solution.py:129
  158.0 1.2 slice_bitcast_fusion
  159.2 1.5 slice.6
  (3 shorter events, 0.0 us)
Async XLA Ops:
  0.6 65.5 %copy-start = (f32[128,128]{1,0:T(8,128)S(1)}, f32[128,128]{1,0:T(8,128)}, u32[]{:S(2)}) copy-start(f32[128,128]{1,0:T(8,128)} %param.13) | copy-start | bytes 196612
  0.6 65.5 %copy-start.1 = (bf16[128,128]{1,0:T(8,128)(2,1)S(1)}, bf16[128,128]{1,0:T(8,128)(2,1)}, u32[]{:S(2)}) copy-start(bf16[128,128]{1,0:T(8,128)(2,1)} %param.15) | copy-start | bytes 98308
  0.7 65.5 %copy-start.2 = (f32[128]{0:T(128)S(1)}, f32[128]{0:T(128)}, u32[]{:S(2)}) copy-start(f32[128]{0:T(128)} %param.14) | copy-start | bytes 1540

commit v2 on v1

v2 whole, which is shorter than its diff:
```python
import functools
import math

import jax
import jax.numpy as jnp
from jax import lax
from jax.experimental import pallas as pl
from jax.experimental.pallas import tpu as pltpu
from jax.sharding import PartitionSpec as P

MESH = pl.DeviceIdType.MESH
CHUNK = 16
INNER = {"row": 2, "col": 4}


def product_kernel(transposed, out_blocks, dest_ref, from_ref, count_ref, values_ref, source_ref, out_ref, totals):
    step = pl.program_id(0)
    live = count_ref[0]

    @pl.when(step == 0)
    def _():
        totals[...] = jnp.zeros_like(totals)

    @pl.when(step * CHUNK < live)
    def _():
        for k in range(CHUNK):
            slot = step * CHUNK + k
            dest = jnp.where(slot < live, dest_ref[slot], out_blocks)
            block = values_ref[k]
            source = source_ref[from_ref[slot]]
            if transposed:
                part = jnp.dot(source, block, preferred_element_type=jnp.float32)
            else:
                part = jnp.dot(block, source, preferred_element_type=jnp.float32)
            totals[dest] += part

    @pl.when(step == pl.num_programs(0) - 1)
    def _():
        out_ref[...] = totals[0:out_blocks].astype(out_ref.dtype)


def tile_product(values, dest, source_of, count, source, out_blocks, transposed, out_dtype):
    slots, size, _ = values.shape
    width = source.shape[2]
    return pl.pallas_call(
        functools.partial(product_kernel, transposed, out_blocks),
        grid_spec=pltpu.PrefetchScalarGridSpec(
            num_scalar_prefetch=3,
            grid=(slots // CHUNK,),
            in_specs=[
                pl.BlockSpec((CHUNK, size, size), lambda i, *_: (i, 0, 0)),
                pl.BlockSpec(source.shape, lambda i, *_: (0, 0, 0)),
            ],
            out_specs=pl.BlockSpec((out_blocks, size, width), lambda i, *_: (0, 0, 0)),
            scratch_shapes=[pltpu.VMEM((out_blocks + 1, size, width), jnp.float32)],
        ),
        out_shape=jax.ShapeDtypeStruct((out_blocks, size, width), out_dtype),
        compiler_params=pltpu.CompilerParams(dimension_semantics=("arbitrary",)),
    )(dest, source_of, count, values, source)


class Group:
    def __init__(self, axis):
        self.axis = axis
        self.n = lax.axis_size(axis)
        self.inner = INNER[axis]
        self.outer = self.n // self.inner
        self.me = lax.axis_index(axis)
        self.o = self.me // self.inner
        self.i = lax.rem(self.me, self.inner)
        self.row, self.col = lax.axis_index("row"), lax.axis_index("col")

    def device(self, peer):
        return (self.row, peer) if self.axis == "col" else (peer, self.col)

    def others_outer(self, k):
        half = k // 2 + 1
        return lax.rem(self.o + jnp.where(k % 2 == 0, half, self.outer - half), self.outer)

    def others_inner(self):
        return [lax.rem(self.i + d, self.inner) for d in range(1, self.inner)]

    def partner(self, k):
        half = k // 2 + 1
        return lax.rem(self.me + jnp.where(k % 2 == 0, half, self.n - half), self.n)

    def copy(self, src, dst, send, recv, peer):
        return pltpu.make_async_remote_copy(
            src_ref=src, dst_ref=dst, send_sem=send, recv_sem=recv,
            device_id=self.device(peer), device_id_type=MESH,
        )

    def hello(self, every):
        barrier = pltpu.get_barrier_semaphore()

        def greet(peer):
            pl.semaphore_signal(barrier, inc=1, device_id=self.device(peer), device_id_type=MESH)

        if every:

            @pl.loop(0, self.n - 1)
            def _(k):
                greet(self.partner(k))

            return self.n - 1

        @pl.loop(0, self.outer - 1)
        def _(k):
            greet(self.others_outer(k) * self.inner + self.i)

        for i in self.others_inner():
            greet(self.o * self.inner + i)
        return self.outer - 1 + self.inner - 1


class Gather:
    def __init__(self, group, src, held, send, recv):
        self.g, self.src, self.held, self.send, self.recv = group, src, held, send, recv

    def to_outer(self, o):
        g = self.g
        peer = o * g.inner + g.i
        return g.copy(self.src, self.held.at[g.me], self.send.at[peer], self.recv.at[g.me], peer)

    def from_slot(self, slot, peer):
        return self.g.copy(self.src, self.held.at[slot], self.send.at[slot], self.recv.at[slot], peer)

    def forward(self, o, i):
        g = self.g
        slot = o * g.inner + g.i
        return g.copy(self.held.at[slot], self.held.at[slot], self.send.at[o * g.inner + i],
                      self.recv.at[slot], g.o * g.inner + i)

    def own_inner(self, i):
        g = self.g
        peer = g.o * g.inner + i
        return g.copy(self.src, self.held.at[g.me], self.send.at[peer], self.recv.at[g.me], peer)

    def start(self):
        g = self.g

        @pl.loop(0, g.outer - 1)
        def _(k):
            self.to_outer(g.others_outer(k)).start()

        for i in g.others_inner():
            self.own_inner(i).start()

    def relay(self):
        g = self.g

        @pl.loop(0, g.outer - 1)
        def _(k):
            o = g.others_outer(k)
            slot = o * g.inner + g.i
            self.from_slot(slot, slot).wait_recv()
            for i in g.others_inner():
                self.forward(o, i).start()

    def finish(self):
        g = self.g
        for i in g.others_inner():
            peer = g.o * g.inner + i
            self.from_slot(peer, peer).wait_recv()

        @pl.loop(0, g.outer - 1)
        def _(k):
            o = g.others_outer(k)
            for i in g.others_inner():
                slot = o * g.inner + i
                self.from_slot(slot, g.o * g.inner + i).wait_recv()

    def drain(self):
        g = self.g

        @pl.loop(0, g.outer - 1)
        def _(k):
            o = g.others_outer(k)
            self.to_outer(o).wait_send()
            for i in g.others_inner():
                self.forward(o, i).wait_send()

        for i in g.others_inner():
            self.own_inner(i).wait_send()


class Scatter:
    def __init__(self, group, src, near, sums, far, send1, recv1, send2, recv2):
        self.g, self.src, self.near, self.sums, self.far = group, src, near, sums, far
        self.send1, self.recv1, self.send2, self.recv2 = send1, recv1, send2, recv2

    def along_inner(self, o, i):
        g = self.g
        slot = o * g.inner + i
        return g.copy(self.src.at[slot], self.near.at[o * g.inner + g.i], self.send1.at[slot],
                      self.recv1.at[o * g.inner + g.i], g.o * g.inner + i)

    def arrived_inner(self, o, i):
        g = self.g
        slot = o * g.inner + i
        return g.copy(self.src.at[slot], self.near.at[slot], self.send1.at[slot], self.recv1.at[slot],
                      g.o * g.inner + i)

    def along_outer(self, o):
        g = self.g
        return g.copy(self.sums.at[o], self.far.at[g.o], self.send2.at[o], self.recv2.at[g.o], o * g.inner + g.i)

    def arrived_outer(self, o):
        g = self.g
        return g.copy(self.sums.at[o], self.far.at[o], self.send2.at[o], self.recv2.at[o], o * g.inner + g.i)

    def start(self):
        g = self.g

        @pl.loop(0, g.outer - 1)
        def _(k):
            for i in g.others_inner():
                self.along_inner(g.others_outer(k), i).start()

        for i in g.others_inner():
            self.along_inner(g.o, i).start()

    def near_sum(self, o):
        g = self.g
        for i in g.others_inner():
            self.arrived_inner(o, i).wait_recv()
        total = self.src[o * g.inner + g.i].astype(jnp.float32)
        for i in g.others_inner():
            total += self.near[o * g.inner + i].astype(jnp.float32)
        return total

    def relay(self):
        g = self.g

        @pl.loop(0, g.outer - 1)
        def _(k):
            o = g.others_outer(k)
            self.sums[o] = self.near_sum(o)
            self.along_outer(o).start()

    def finish(self):
        g = self.g
        own = self.near_sum(g.o)

        def add(k, total):
            o = g.others_outer(k)
            self.arrived_outer(o).wait_recv()
            return total + self.far[o]

        return lax.fori_loop(0, g.outer - 1, add, own)

    def drain(self):
        g = self.g

        @pl.loop(0, g.outer - 1)
        def _(k):
            o = g.others_outer(k)
            self.along_outer(o).wait_send()
            for i in g.others_inner():
                self.along_inner(o, i).wait_send()

        for i in g.others_inner():
            self.along_inner(g.o, i).wait_send()


def gather_kernel(axis, src, out, held, send, recv):
    g = Group(axis)
    gather = Gather(g, src, held, send, recv)
    pl.semaphore_wait(pltpu.get_barrier_semaphore(), g.hello(False))
    gather.start()
    held[g.me] = src[...]
    gather.relay()
    gather.finish()
    out[...] = held[...]
    gather.drain()


def scatter_kernel(axis, src, out, near, sums, far, send1, recv1, send2, recv2):
    g = Group(axis)
    scatter = Scatter(g, src, near, sums, far, send1, recv1, send2, recv2)
    pl.semaphore_wait(pltpu.get_barrier_semaphore(), g.hello(False))
    scatter.start()
    scatter.relay()
    out[...] = scatter.finish()
    scatter.drain()


def middle_kernel(src, slices, out, slice_out, held, send, recv, near, sums, far, send1, recv1, send2, recv2):
    g = Group("col")
    gather = Gather(g, src, held, send, recv)
    scatter = Scatter(g, slices, near, sums, far, send1, recv1, send2, recv2)
    pl.semaphore_wait(pltpu.get_barrier_semaphore(), g.hello(False))
    gather.start()
    scatter.start()
    held[g.me] = src[...]
    gather.relay()
    scatter.relay()
    slice_out[...] = scatter.finish()
    gather.finish()
    out[...] = held[...]
    gather.drain()
    scatter.drain()


def last_kernel(back, part, out, all_out, held, held_part, own, held_all, sb, rb, sp, rp, sa, ra):
    g, c = Group("row"), Group("col")
    gather = Gather(c, own, held_all, sa, ra)

    def block(peer, slot):
        return g.copy(back.at[peer], held.at[slot], sb.at[peer], rb.at[slot], peer)

    def piece(peer, slot):
        return g.copy(part, held_part.at[slot], sp.at[peer], rp.at[slot], peer)

    pl.semaphore_wait(pltpu.get_barrier_semaphore(), g.hello(True) + c.hello(False))

    @pl.loop(0, g.n - 1)
    def _(k):
        piece(g.partner(k), g.me).start()

    @pl.loop(0, g.n - 1)
    def _(k):
        block(g.partner(k), g.me).start()

    held_part[g.me] = part[...]

    @pl.loop(0, g.n - 1)
    def _(k):
        piece(g.partner(k), g.partner(k)).wait_recv()

    total = held_part[0]
    for s in range(1, g.n):
        total += held_part[s]
    own[...] = total
    held_all[c.me] = total
    gather.start()

    def add(k, total):
        block(g.partner(k), g.partner(k)).wait_recv()
        return total + held[g.partner(k)].astype(jnp.float32)

    gather.relay()
    out[...] = lax.fori_loop(0, g.n - 1, add, back[g.me].astype(jnp.float32))
    gather.finish()
    all_out[...] = held_all[...]
    gather.drain()

    @pl.loop(0, g.n - 1)
    def _(k):
        block(g.partner(k), g.partner(k)).wait_send()
        piece(g.partner(k), g.partner(k)).wait_send()


def call(kernel, number, outs, scratch, *arrays):
    vmem = pl.BlockSpec(memory_space=pltpu.VMEM)
    return pl.pallas_call(
        kernel,
        out_shape=outs,
        in_specs=[vmem] * len(arrays),
        out_specs=[vmem] * len(outs),
        scratch_shapes=scratch,
        compiler_params=pltpu.CompilerParams(collective_id=number, has_side_effects=True),
    )(*arrays)


def copies(*sizes):
    return [pltpu.SemaphoreType.DMA((size,)) for size in sizes]


def gather_scratch(n, block, dtype):
    return [pltpu.VMEM((n,) + block, dtype)] + copies(n, n)


def scatter_scratch(axis, block, dtype):
    n = lax.axis_size(axis)
    outer = n // INNER[axis]
    return [
        pltpu.VMEM((n,) + block, dtype),
        pltpu.VMEM((outer,) + block, jnp.float32),
        pltpu.VMEM((outer,) + block, jnp.float32),
    ] + copies(n, n, outer, outer)


def per_device(features, block_values, block_rows, block_cols, counts, weight, bias, cotangent):
    size, width = features.shape
    hidden_width = weight.shape[1]
    row_count = lax.axis_size("row")
    col_count = lax.axis_size("col")
    values = block_values[0, 0]
    rows = block_rows[0, 0]
    cols = block_cols[0, 0]
    count = counts[0]

    shape = jax.ShapeDtypeStruct
    block = (size, width)
    (column_feats,) = call(
        functools.partial(gather_kernel, "row"), 0, [shape((row_count,) + block, features.dtype)],
        gather_scratch(row_count, block, features.dtype), features,
    )
    partial = tile_product(values, rows, cols, count, column_feats, col_count, False, jnp.bfloat16)
    (aggregated,) = call(
        functools.partial(scatter_kernel, "col"), 1, [shape(block, jnp.float32)],
        scatter_scratch("col", block, partial.dtype), partial,
    )

    highest = lax.Precision.HIGHEST
    pre_act = jnp.dot(aggregated, weight, precision=highest) + bias[None, :]
    sigm = 1.0 / (1.0 + jnp.exp(-pre_act))
    hidden = pre_act * sigm
    masked_grad = cotangent.astype(jnp.float32) * sigm * (1.0 + pre_act * (1.0 - sigm))
    grad_own = lax.dot_general(
        weight, masked_grad, (((1,), (1,)), ((), ())), precision=highest
    ).astype(jnp.bfloat16)
    norm_factor = 1.0 / math.sqrt(size * row_count * col_count)
    weight_part = jnp.dot(aggregated.T, masked_grad, precision=highest) * norm_factor
    bias_part = jnp.sum(masked_grad, axis=0) * norm_factor
    per_slice = width // col_count
    slices = jnp.concatenate(
        [
            weight_part.reshape(col_count, per_slice, hidden_width),
            jnp.broadcast_to(bias_part, (col_count, 1, hidden_width)),
            jnp.zeros((col_count, -(per_slice + 1) % 8, hidden_width), jnp.float32),
        ],
        axis=1,
    )

    piece = slices.shape[1:]
    grad_row, col_slice = call(
        middle_kernel, 2, [shape((col_count,) + grad_own.shape, grad_own.dtype), shape(piece, jnp.float32)],
        gather_scratch(col_count, grad_own.shape, grad_own.dtype) + scatter_scratch("col", piece, jnp.float32),
        grad_own, slices,
    )
    back = tile_product(values, cols, rows, count, grad_row, row_count, True, jnp.bfloat16)
    grad_t, all_slices = call(
        last_kernel, 3, [shape(back.shape[1:], jnp.float32), shape((col_count,) + piece, jnp.float32)],
        [
            pltpu.VMEM(back.shape, back.dtype),
            pltpu.VMEM((row_count,) + piece, jnp.float32),
            pltpu.VMEM(piece, jnp.float32),
            pltpu.VMEM((col_count,) + piece, jnp.float32),
        ]
        + copies(row_count, row_count, row_count, row_count, col_count, col_count),
        back, col_slice,
    )
    grad_weight = all_slices[:, :per_slice].reshape(width, hidden_width)
    grad_bias = all_slices[0, per_slice]
    return (hidden, grad_t.T, grad_weight, grad_bias)


def solution(mesh):
    placed = (
        P(("row", "col"), None),
        P("row", "col", None, None, None),
        P("row", "col", None),
        P("row", "col", None),
        P("row", "col"),
        P(),
        P(),
        P(("row", "col"), None),
    )
    return jax.shard_map(
        per_device,
        mesh=mesh,
        in_specs=placed,
        out_specs=(P(("row", "col"), None), P(("row", "col"), None), P(), P()),
        check_vma=False,
    )
```

time: 162 us -> 124 us (0.77)
  Pallas kernels: 150 us -> 113 us
    pallas_call x5 -> x4, Pallas kernels: 135 us -> 99.2 us  [call(): pl.pallas_call(kernel, out_shape=outs, in_specs=[vmem] * len(arrays), out...]
    pallas_call x2, Pallas kernels: 15.2 us -> 13.4 us  [tile_product(): pl.pallas_call(functools.partial(product_kernel, transposed, out_blocks),...]
where the time goes in v2:
time: 124 us; the launch traced here: 123 us
  Pallas kernels  113 us (91%)
  local copies, waits for them, and re-layouts  4.4 us (4%)
  matrix products  3.71 us (3%)
  between operations  1.43 us (1%)
    pallas_call x4, Pallas kernels, call(): pl.pallas_call(kernel, out_shape=outs, in_specs=[vmem] * len(arrays), out...  99.2 us
    pallas_call x2, Pallas kernels, tile_product(): pl.pallas_call(functools.partial(product_kernel, transposed, out_blocks),...  13.4 us

profile of v2, /device:TPU:1, one launch (start us, length us, event | category | flops | bytes accessed | tf_op | source)
XLA Modules:
  0.0 122.9 jit_solution(12350154746103084238)
XLA Ops:
  0.6 0.0 copy-start
  0.6 0.0 copy-start.1
  0.7 0.0 copy-start.2
  1.4 0.1 pad.2.clone
  1.4 20.5 %shard_map.111.source_ref = bf16[16,128,128]{2,1,0:T(8,128)(2,1)} custom-call(bf16[128,128]{1,0:T(8,128)(2,1)} %src.1), custom_call_target="tpu_custom_call" | custom-call | tf_op jit(solution)/shard_map/pallas_call | solution.py:356
  22.0 6.8 %shard_map.112.src = bf16[32,128,128]{2,1,0:T(8,128)(2,1)} custom-call(s32[128]{0:T(128)} %bitcast.24, s32[128]{0:T(128)} %bitcast.26, s32[1]{0:T(128)} %bitcast.17.count_ref, bf16[128,128,128]{2,1,0:T(8,128)(2,1)} %bitcast.19, bf16[16,128,128]{2,1,0:T(8,128)(2,1)} %shard_map.111.source_ref), custom_call_target="tpu_custom_call" | custom-call | tf_op jit(solution)/shard_map/pallas_call | solution.py:45
  28.7 28.8 %shard_map.113 = f32[128,128]{1,0:T(8,128)} custom-call(bf16[32,128,128]{2,1,0:T(8,128)(2,1)} %shard_map.112.src), custom_call_target="tpu_custom_call" | custom-call | tf_op jit(solution)/shard_map/pallas_call | solution.py:356
  57.6 0.0 copy-done
  57.6 0.0 copy-done.1
  57.6 0.0 copy-done.2
  57.6 1.7 %fusion.2 = (f32[128]{0:T(128)S(1)}, f32[128,128]{1,0:T(8,128)S(1)}, f32[128,128]{1,0:T(8,128)}) fusion(bf16[128,128]{1,0:T(8,128)(2,1)S(1)} %copy-done.1, f32[128]{0:T(128)S(1)} %copy-done.2, f32[128,128]{1,0:T(8,128)} %shard_map.113, f32[128,128]{1,0:T(8,128)S(1)} %copy-done), kind=kOutput, calls=%fused_computation.10 | convolution fusion | flops 25362304 | bytes 295936 | tf_op jit(solution)/shard_map/dot_general | solution.py:407
  59.3 1.1 convolution_multiply_fusion
  60.5 0.9 fusion.src
  61.4 0.7 maximum_maximum_fusion.slices
  62.1 23.8 %shard_map.114 = (bf16[32,128,128]{2,1,0:T(8,128)(2,1)}, f32[8,128]{1,0:T(8,128)}) custom-call(bf16[128,128]{1,0:T(8,128)(2,1)} %fusion.src, f32[32,8,128]{2,1,0:T(8,128)} %maximum_maximum_fusion.slices), custom_call_target="tpu_custom_call" | custom-call | tf_op jit(solution)/shard_map/pallas_call | solution.py:356
  85.9 6.7 %shard_map.115.back = bf16[16,128,128]{2,1,0:T(8,128)(2,1)} custom-call(s32[128]{0:T(128)} %bitcast.27, s32[128]{0:T(128)} %bitcast.25, s32[1]{0:T(128)} %bitcast.18.count_ref, bf16[128,128,128]{2,1,0:T(8,128)(2,1)} %bitcast.20, bf16[32,128,128]{2,1,0:T(8,128)(2,1)} %get-tuple-element.8.source_ref), custom_call_target="tpu_custom_call" | custom-call | tf_op jit(solution)/shard_map/pallas_call | solution.py:45
  92.5 26.1 %shard_map.116 = (f32[128,128]{1,0:T(8,128)}, f32[32,8,128]{2,1,0:T(8,128)}) custom-call(bf16[16,128,128]{2,1,0:T(8,128)(2,1)} %shard_map.115.back, f32[8,128]{1,0:T(8,128)} %get-tuple-element.9.part), custom_call_target="tpu_custom_call" | custom-call | tf_op jit(solution)/shard_map/pallas_call | solution.py:356
  118.6 1.6 %copy.13 = f32[128,128]{1,0:T(8,128)} copy(f32[128,128]{0,1:T(8,128)} %bitcast.23) | data formatting | bytes 131072
  120.2 1.2 slice_bitcast_fusion
  121.4 1.5 %slice.6 = f32[32,4,128]{2,1,0:T(4,128)} slice(f32[32,8,128]{2,1,0:T(8,128)} %get-tuple-element.11), slice={[0:32], [0:4], [0:128]} | slice | bytes 131072 | tf_op jit(solution)/shard_map/slice | solution.py:445
  (3 shorter events, 0.0 us)
Async XLA Ops:
  0.6 57.0 %copy-start = (f32[128,128]{1,0:T(8,128)S(1)}, f32[128,128]{1,0:T(8,128)}, u32[]{:S(2)}) copy-start(f32[128,128]{1,0:T(8,128)} %param.13) | copy-start | bytes 196612
  0.6 56.9 %copy-start.1 = (bf16[128,128]{1,0:T(8,128)(2,1)S(1)}, bf16[128,128]{1,0:T(8,128)(2,1)}, u32[]{:S(2)}) copy-start(bf16[128,128]{1,0:T(8,128)(2,1)} %param.15) | copy-start | bytes 98308
  0.7 56.9 %copy-start.2 = (f32[128]{0:T(128)S(1)}, f32[128]{0:T(128)}, u32[]{:S(2)}) copy-start(f32[128]{0:T(128)} %param.14) | copy-start | bytes 1540

commit v3 on v2

--- a/solution.py
+++ b/solution.py
@@ -143,8 +143,37 @@
         def _(k):
             self.to_outer(g.others_outer(k)).start()
 
-        for i in g.others_inner():
+        for i in self.near():
             self.own_inner(i).start()
+
+    def near(self):
+        g = self.g
+        if g.inner == 4:
+            return [lax.rem(g.i + 1, 4), lax.rem(g.i + 3, 4)]
+        return g.others_inner()
+
+    def second(self, o):
+        g = self.g
+        even = lax.rem(o, 2) == 0
+        source = lax.rem(g.i + jnp.where(even, 3, 1), 4)
+        target = lax.rem(g.i + jnp.where(even, 1, 3), 4)
+        opposite = lax.rem(g.i + 2, 4)
+        slot = o * g.inner + source
+        return g.copy(self.held.at[slot], self.held.at[slot], self.send.at[o * g.inner + opposite],
+                      self.recv.at[slot], g.o * g.inner + target), source, target
+
+    def pass_on(self, o):
+        g = self.g
+        if g.inner == 4:
+            copy, source, _ = self.second(o)
+            self.from_slot(o * g.inner + source, g.o * g.inner + source).wait_recv()
+            copy.start()
+
+    def remaining(self, o):
+        g = self.g
+        if g.inner == 4:
+            return [self.second(o)[2], lax.rem(g.i + 2, 4)]
+        return g.others_inner()
 
     def relay(self):
         g = self.g
@@ -154,19 +183,22 @@
             o = g.others_outer(k)
             slot = o * g.inner + g.i
             self.from_slot(slot, slot).wait_recv()
-            for i in g.others_inner():
+            for i in self.near():
                 self.forward(o, i).start()
+            self.pass_on(jnp.where(k == 0, g.o, g.others_outer(jnp.maximum(k - 1, 0))))
+
+        self.pass_on(g.others_outer(g.outer - 2) if g.outer > 1 else g.o)
 
     def finish(self):
         g = self.g
-        for i in g.others_inner():
+        for i in self.remaining(g.o):
             peer = g.o * g.inner + i
             self.from_slot(peer, peer).wait_recv()
 
         @pl.loop(0, g.outer - 1)
         def _(k):
             o = g.others_outer(k)
-            for i in g.others_inner():
+            for i in self.remaining(o):
                 slot = o * g.inner + i
                 self.from_slot(slot, g.o * g.inner + i).wait_recv()
 
@@ -177,11 +209,15 @@
         def _(k):
             o = g.others_outer(k)
             self.to_outer(o).wait_send()
-            for i in g.others_inner():
+            for i in self.near():
                 self.forward(o, i).wait_send()
-
-        for i in g.others_inner():
+            if g.inner == 4:
+                self.second(o)[0].wait_send()
+
+        for i in self.near():
             self.own_inner(i).wait_send()
+        if g.inner == 4:
+            self.second(g.o)[0].wait_send()
 
 
 class Scatter:
@@ -275,31 +311,58 @@
     gather.drain()
 
 
-def scatter_kernel(axis, src, out, near, sums, far, send1, recv1, send2, recv2):
-    g = Group(axis)
-    scatter = Scatter(g, src, near, sums, far, send1, recv1, send2, recv2)
+def middle_kernel(
+    per_slice, norm_factor, part, weight, bias, cotangent,
+    hidden_out, out, slice_out,
+    near, sums, far, send1, recv1, send2, recv2,
+    own, slices, held, send, recv,
+    near_b, sums_b, far_b, send1_b, recv1_b, send2_b, recv2_b,
+):
+    g = Group("col")
+    scatter = Scatter(g, part, near, sums, far, send1, recv1, send2, recv2)
+    gather = Gather(g, own, held, send, recv)
+    small = Scatter(g, slices, near_b, sums_b, far_b, send1_b, recv1_b, send2_b, recv2_b)
     pl.semaphore_wait(pltpu.get_barrier_semaphore(), g.hello(False))
     scatter.start()
     scatter.relay()
-    out[...] = scatter.finish()
-    scatter.drain()
-
-
-def middle_kernel(src, slices, out, slice_out, held, send, recv, near, sums, far, send1, recv1, send2, recv2):
-    g = Group("col")
-    gather = Gather(g, src, held, send, recv)
-    scatter = Scatter(g, slices, near, sums, far, send1, recv1, send2, recv2)
-    pl.semaphore_wait(pltpu.get_barrier_semaphore(), g.hello(False))
+    aggregated = scatter.finish()
+
+    highest = lax.Precision.HIGHEST
+    pre_act = jnp.dot(aggregated, weight[...], precision=highest, preferred_element_type=jnp.float32) + bias[...]
+    sigm = 1.0 / (1.0 + jnp.exp(-pre_act))
+    masked_grad = cotangent[...].astype(jnp.float32) * sigm * (1.0 + pre_act * (1.0 - sigm))
+    grad_t = lax.dot_general(
+        weight[...], masked_grad, (((1,), (1,)), ((), ())), precision=highest, preferred_element_type=jnp.float32
+    ).astype(own.dtype)
+    own[...] = grad_t
+    held[g.me] = grad_t
+    hidden_out[...] = pre_act * sigm
+    bias_part = jnp.sum(masked_grad, axis=0, keepdims=True) * norm_factor
     gather.start()
-    scatter.start()
-    held[g.me] = src[...]
+    weight_part = norm_factor * lax.dot_general(
+        aggregated, masked_grad, (((0,), (0,)), ((), ())), precision=highest, preferred_element_type=jnp.float32
+    )
+    spare = slices.shape[1] - per_slice
+    for s in range(g.n):
+        slices[s, 0:per_slice] = weight_part[s * per_slice : (s + 1) * per_slice]
+        slices[s, per_slice:] = jnp.broadcast_to(bias_part, (spare, bias_part.shape[1]))
     gather.relay()
-    scatter.relay()
-    slice_out[...] = scatter.finish()
+    small.start()
+    small.relay()
+    slice_out[...] = small.finish()
     gather.finish()
     out[...] = held[...]
+    scatter.drain()
     gather.drain()
-    scatter.drain()
+    small.drain()
+
+
+def output_kernel(per_slice, hidden, grad_t, slices, hidden_out, grad_out, weight_out, bias_out):
+    hidden_out[...] = hidden[...]
+    grad_out[...] = grad_t[...].T
+    for s in range(slices.shape[0]):
+        weight_out[s * per_slice : (s + 1) * per_slice] = slices[s, 0:per_slice]
+    bias_out[...] = slices[0, per_slice : per_slice + 1]
 
 
 def last_kernel(back, part, out, all_out, held, held_part, own, held_all, sb, rb, sp, rp, sa, ra):
@@ -398,37 +461,21 @@
         gather_scratch(row_count, block, features.dtype), features,
     )
     partial = tile_product(values, rows, cols, count, column_feats, col_count, False, jnp.bfloat16)
-    (aggregated,) = call(
-        functools.partial(scatter_kernel, "col"), 1, [shape(block, jnp.float32)],
-        scatter_scratch("col", block, partial.dtype), partial,
-    )
-
-    highest = lax.Precision.HIGHEST
-    pre_act = jnp.dot(aggregated, weight, precision=highest) + bias[None, :]
-    sigm = 1.0 / (1.0 + jnp.exp(-pre_act))
-    hidden = pre_act * sigm
-    masked_grad = cotangent.astype(jnp.float32) * sigm * (1.0 + pre_act * (1.0 - sigm))
-    grad_own = lax.dot_general(
-        weight, masked_grad, (((1,), (1,)), ((), ())), precision=highest
-    ).astype(jnp.bfloat16)
     norm_factor = 1.0 / math.sqrt(size * row_count * col_count)
-    weight_part = jnp.dot(aggregated.T, masked_grad, precision=highest) * norm_factor
-    bias_part = jnp.sum(masked_grad, axis=0) * norm_factor
     per_slice = width // col_count
-    slices = jnp.concatenate(
+    piece = (per_slice + 1 + -(per_slice + 1) % 8, hidden_width)
+    hidden, grad_row, col_slice = call(
+        functools.partial(middle_kernel, per_slice, norm_factor), 2,
         [
-            weight_part.reshape(col_count, per_slice, hidden_width),
-            jnp.broadcast_to(bias_part, (col_count, 1, hidden_width)),
-            jnp.zeros((col_count, -(per_slice + 1) % 8, hidden_width), jnp.float32),
+            shape((size, hidden_width), jnp.float32),
+            shape((col_count, width, size), jnp.bfloat16),
+            shape(piece, jnp.float32),
         ],
-        axis=1,
-    )
-
-    piece = slices.shape[1:]
-    grad_row, col_slice = call(
-        middle_kernel, 2, [shape((col_count,) + grad_own.shape, grad_own.dtype), shape(piece, jnp.float32)],
-        gather_scratch(col_count, grad_own.shape, grad_own.dtype) + scatter_scratch("col", piece, jnp.float32),
-        grad_own, slices,
+        scatter_scratch("col", block, partial.dtype)
+        + [pltpu.VMEM((width, size), jnp.bfloat16), pltpu.VMEM((col_count,) + piece, jnp.float32)]
+        + gather_scratch(col_count, (width, size), jnp.bfloat16)
+        + scatter_scratch("col", piece, jnp.float32),
+        partial, weight, bias[None, :], cotangent,
     )
     back = tile_product(values, cols, rows, count, grad_row, row_count, True, jnp.bfloat16)
     grad_t, all_slices = call(
@@ -442,9 +489,19 @@
         + copies(row_count, row_count, row_count, row_count, col_count, col_count),
         back, col_slice,
     )
-    grad_weight = all_slices[:, :per_slice].reshape(width, hidden_width)
-    grad_bias = all_slices[0, per_slice]
-    return (hidden, grad_t.T, grad_weight, grad_bias)
+    vmem = pl.BlockSpec(memory_space=pltpu.VMEM)
+    hidden, grad_features, grad_weight, grad_bias = pl.pallas_call(
+        functools.partial(output_kernel, per_slice),
+        out_shape=[
+            shape(hidden.shape, jnp.float32),
+            shape(block, jnp.float32),
+            shape((width, hidden_width), jnp.float32),
+            shape((1, hidden_width), jnp.float32),
+        ],
+        in_specs=[vmem] * 3,
+        out_specs=[vmem] * 4,
+    )(hidden, grad_t, all_slices)
+    return (hidden, grad_features, grad_weight, grad_bias[0])
 
 
 def solution(mesh):

time: 124 us -> 132 us (1.065)
  the two profiles are of different devices: /device:TPU:1 before, /device:TPU:10 now
where the time goes in v3:
time: 132 us
  Pallas kernels  130 us (98%)
    pallas_call x3, Pallas kernels, call(): pl.pallas_call(kernel, out_shape=outs, in_specs=[vmem] * len(arrays), out...  114 us
    pallas_call x2, Pallas kernels, tile_product(): pl.pallas_call(functools.partial(product_kernel, transposed, out_blocks),...  14.5 us

profile of v3, /device:TPU:10, one launch (start us, length us, event | category | flops | bytes accessed | tf_op | source)
XLA Modules:
  0.0 131.8 jit_solution(6708317727645960432)
XLA Ops:
  1.3 15.7 %shard_map.111.source_ref = bf16[16,128,128]{2,1,0:T(8,128)(2,1)} custom-call(bf16[128,128]{1,0:T(8,128)(2,1)} %src.1), custom_call_target="tpu_custom_call" | custom-call | tf_op jit(solution)/shard_map/pallas_call | solution.py:419
  17.0 7.3 %shard_map.112.part = bf16[32,128,128]{2,1,0:T(8,128)(2,1)} custom-call(s32[128]{0:T(128)} %bitcast.10, s32[128]{0:T(128)} %bitcast.12, s32[1]{0:T(128)} %bitcast.6.count_ref, bf16[128,128,128]{2,1,0:T(8,128)(2,1)} %bitcast.8, bf16[16,128,128]{2,1,0:T(8,128)(2,1)} %shard_map.111.source_ref), custom_call_target="tpu_custom_call" | custom-call | tf_op jit(solution)/shard_map/pallas_call | solution.py:45
  24.3 65.6 %shard_map.113 = (f32[128,128]{1,0:T(8,128)}, bf16[32,128,128]{2,1,0:T(8,128)(2,1)}, f32[8,128]{1,0:T(8,128)}) custom-call(bf16[32,128,128]{2,1,0:T(8,128)(2,1)} %shard_map.112.part, f32[128,128]{1,0:T(8,128)} %weight.1, f32[1,128]{1,0:T(1,128)} %bitcast.14, bf16[128,128]{1,0:T(8,128)(2,1)} %cotangent.1), custom_call_target="tpu_custom_call" | custom-call | tf_op jit(solution)/shard_map/pallas_call | solution.py:419
  89.9 7.2 %shard_map.114.back = bf16[16,128,128]{2,1,0:T(8,128)(2,1)} custom-call(s32[128]{0:T(128)} %bitcast.13, s32[128]{0:T(128)} %bitcast.11, s32[1]{0:T(128)} %bitcast.7.count_ref, bf16[128,128,128]{2,1,0:T(8,128)(2,1)} %bitcast.9, bf16[32,128,128]{2,1,0:T(8,128)(2,1)} %get-tuple-element.14.source_ref), custom_call_target="tpu_custom_call" | custom-call | tf_op jit(solution)/shard_map/pallas_call | solution.py:45
  97.1 32.9 %shard_map.115 = (f32[128,128]{1,0:T(8,128)}, f32[32,8,128]{2,1,0:T(8,128)}) custom-call(bf16[16,128,128]{2,1,0:T(8,128)(2,1)} %shard_map.114.back, f32[8,128]{1,0:T(8,128)} %get-tuple-element.15.part), custom_call_target="tpu_custom_call" | custom-call | tf_op jit(solution)/shard_map/pallas_call | solution.py:419
  130.0 1.7 %shard_map.116 = (f32[128,128]{1,0:T(8,128)}, f32[128,128]{1,0:T(8,128)}, f32[128,128]{1,0:T(8,128)}, f32[1,128]{1,0:T(1,128)}) custom-call(f32[128,128]{1,0:T(8,128)} %get-tuple-element.13.hidden, f32[128,128]{1,0:T(8,128)} %get-tuple-element.16.grad_t, f32[32,8,128]{2,1,0:T(8,128)} %get-tuple-element.17.slices), custom_call_target="tpu_custom_call" | custom-call | tf_op jit(solution)/shard_map/pallas_call | solution.py:493

commit v4 on v3

--- a/solution.py
+++ b/solution.py
@@ -143,37 +143,8 @@
         def _(k):
             self.to_outer(g.others_outer(k)).start()
 
-        for i in self.near():
+        for i in g.others_inner():
             self.own_inner(i).start()
-
-    def near(self):
-        g = self.g
-        if g.inner == 4:
-            return [lax.rem(g.i + 1, 4), lax.rem(g.i + 3, 4)]
-        return g.others_inner()
-
-    def second(self, o):
-        g = self.g
-        even = lax.rem(o, 2) == 0
-        source = lax.rem(g.i + jnp.where(even, 3, 1), 4)
-        target = lax.rem(g.i + jnp.where(even, 1, 3), 4)
-        opposite = lax.rem(g.i + 2, 4)
-        slot = o * g.inner + source
-        return g.copy(self.held.at[slot], self.held.at[slot], self.send.at[o * g.inner + opposite],
-                      self.recv.at[slot], g.o * g.inner + target), source, target
-
-    def pass_on(self, o):
-        g = self.g
-        if g.inner == 4:
-            copy, source, _ = self.second(o)
-            self.from_slot(o * g.inner + source, g.o * g.inner + source).wait_recv()
-            copy.start()
-
-    def remaining(self, o):
-        g = self.g
-        if g.inner == 4:
-            return [self.second(o)[2], lax.rem(g.i + 2, 4)]
-        return g.others_inner()
 
     def relay(self):
         g = self.g
@@ -183,22 +154,19 @@
             o = g.others_outer(k)
             slot = o * g.inner + g.i
             self.from_slot(slot, slot).wait_recv()
-            for i in self.near():
+            for i in g.others_inner():
                 self.forward(o, i).start()
-            self.pass_on(jnp.where(k == 0, g.o, g.others_outer(jnp.maximum(k - 1, 0))))
-
-        self.pass_on(g.others_outer(g.outer - 2) if g.outer > 1 else g.o)
 
     def finish(self):
         g = self.g
-        for i in self.remaining(g.o):
+        for i in g.others_inner():
             peer = g.o * g.inner + i
             self.from_slot(peer, peer).wait_recv()
 
         @pl.loop(0, g.outer - 1)
         def _(k):
             o = g.others_outer(k)
-            for i in self.remaining(o):
+            for i in g.others_inner():
                 slot = o * g.inner + i
                 self.from_slot(slot, g.o * g.inner + i).wait_recv()
 
@@ -209,15 +177,11 @@
         def _(k):
             o = g.others_outer(k)
             self.to_outer(o).wait_send()
-            for i in self.near():
+            for i in g.others_inner():
                 self.forward(o, i).wait_send()
-            if g.inner == 4:
-                self.second(o)[0].wait_send()
-
-        for i in self.near():
+
+        for i in g.others_inner():
             self.own_inner(i).wait_send()
-        if g.inner == 4:
-            self.second(g.o)[0].wait_send()
 
 
 class Scatter:
@@ -346,12 +310,12 @@
     for s in range(g.n):
         slices[s, 0:per_slice] = weight_part[s * per_slice : (s + 1) * per_slice]
         slices[s, per_slice:] = jnp.broadcast_to(bias_part, (spare, bias_part.shape[1]))
+    small.start()
     gather.relay()
-    small.start()
     small.relay()
-    slice_out[...] = small.finish()
     gather.finish()
     out[...] = held[...]
+    slice_out[...] = small.finish()
     scatter.drain()
     gather.drain()
     small.drain()

time: 132 us -> 115 us (0.87)
  the two profiles are of different devices: /device:TPU:10 before, /device:TPU:8 now
where the time goes in v4:
time: 115 us
  Pallas kernels  113 us (98%)
  between operations  1.3 us (1%)
    pallas_call x3, Pallas kernels, call(): pl.pallas_call(kernel, out_shape=outs, in_specs=[vmem] * len(arrays), out...  97.2 us
    pallas_call x2, Pallas kernels, tile_product(): pl.pallas_call(functools.partial(product_kernel, transposed, out_blocks),...  14.5 us

profile of v4, /device:TPU:8, one launch (start us, length us, event | category | flops | bytes accessed | tf_op | source)
XLA Modules:
  0.0 114.8 jit_solution(4764729751694522878)
XLA Ops:
  1.3 17.8 %shard_map.111.source_ref = bf16[16,128,128]{2,1,0:T(8,128)(2,1)} custom-call(bf16[128,128]{1,0:T(8,128)(2,1)} %src.1), custom_call_target="tpu_custom_call" | custom-call | tf_op jit(solution)/shard_map/pallas_call | solution.py:383
  19.1 7.3 %shard_map.112.part = bf16[32,128,128]{2,1,0:T(8,128)(2,1)} custom-call(s32[128]{0:T(128)} %bitcast.10, s32[128]{0:T(128)} %bitcast.12, s32[1]{0:T(128)} %bitcast.6.count_ref, bf16[128,128,128]{2,1,0:T(8,128)(2,1)} %bitcast.8, bf16[16,128,128]{2,1,0:T(8,128)(2,1)} %shard_map.111.source_ref), custom_call_target="tpu_custom_call" | custom-call | tf_op jit(solution)/shard_map/pallas_call | solution.py:45
  26.4 51.9 %shard_map.113 = (f32[128,128]{1,0:T(8,128)}, bf16[32,128,128]{2,1,0:T(8,128)(2,1)}, f32[8,128]{1,0:T(8,128)}) custom-call(bf16[32,128,128]{2,1,0:T(8,128)(2,1)} %shard_map.112.part, f32[128,128]{1,0:T(8,128)} %weight.1, f32[1,128]{1,0:T(1,128)} %bitcast.14, bf16[128,128]{1,0:T(8,128)(2,1)} %cotangent.1), custom_call_target="tpu_custom_call" | custom-call | tf_op jit(solution)/shard_map/pallas_call | solution.py:383
  78.3 7.2 %shard_map.114.back = bf16[16,128,128]{2,1,0:T(8,128)(2,1)} custom-call(s32[128]{0:T(128)} %bitcast.13, s32[128]{0:T(128)} %bitcast.11, s32[1]{0:T(128)} %bitcast.7.count_ref, bf16[128,128,128]{2,1,0:T(8,128)(2,1)} %bitcast.9, bf16[32,128,128]{2,1,0:T(8,128)(2,1)} %get-tuple-element.14.source_ref), custom_call_target="tpu_custom_call" | custom-call | tf_op jit(solution)/shard_map/pallas_call | solution.py:45
  85.5 27.5 %shard_map.115 = (f32[128,128]{1,0:T(8,128)}, f32[32,8,128]{2,1,0:T(8,128)}) custom-call(bf16[16,128,128]{2,1,0:T(8,128)(2,1)} %shard_map.114.back, f32[8,128]{1,0:T(8,128)} %get-tuple-element.15.part), custom_call_target="tpu_custom_call" | custom-call | tf_op jit(solution)/shard_map/pallas_call | solution.py:383
  113.1 1.7 %shard_map.116 = (f32[128,128]{1,0:T(8,128)}, f32[128,128]{1,0:T(8,128)}, f32[128,128]{1,0:T(8,128)}, f32[1,128]{1,0:T(1,128)}) custom-call(f32[128,128]{1,0:T(8,128)} %get-tuple-element.13.hidden, f32[128,128]{1,0:T(8,128)} %get-tuple-element.16.grad_t, f32[32,8,128]{2,1,0:T(8,128)} %get-tuple-element.17.slices), custom_call_target="tpu_custom_call" | custom-call | tf_op jit(solution)/shard_map/pallas_call | solution.py:457

commit v5 on v4

--- a/solution.py
+++ b/solution.py
@@ -77,6 +77,9 @@
         half = k // 2 + 1
         return lax.rem(self.o + jnp.where(k % 2 == 0, half, self.outer - half), self.outer)
 
+    def far_first(self, k):
+        return self.others_outer(self.outer - 2 - k)
+
     def others_inner(self):
         return [lax.rem(self.i + d, self.inner) for d in range(1, self.inner)]
 
@@ -215,7 +218,7 @@
         @pl.loop(0, g.outer - 1)
         def _(k):
             for i in g.others_inner():
-                self.along_inner(g.others_outer(k), i).start()
+                self.along_inner(g.far_first(k), i).start()
 
         for i in g.others_inner():
             self.along_inner(g.o, i).start()
@@ -234,7 +237,7 @@
 
         @pl.loop(0, g.outer - 1)
         def _(k):
-            o = g.others_outer(k)
+            o = g.far_first(k)
             self.sums[o] = self.near_sum(o)
             self.along_outer(o).start()
 
@@ -243,7 +246,7 @@
         own = self.near_sum(g.o)
 
         def add(k, total):
-            o = g.others_outer(k)
+            o = g.far_first(k)
             self.arrived_outer(o).wait_recv()
             return total + self.far[o]
 
@@ -254,7 +257,7 @@
 
         @pl.loop(0, g.outer - 1)
         def _(k):
-            o = g.others_outer(k)
+            o = g.far_first(k)
             self.along_outer(o).wait_send()
             for i in g.others_inner():
                 self.along_inner(o, i).wait_send()

time: 115 us -> 109 us (0.948)
  the two profiles are of different devices: /device:TPU:8 before, /device:TPU:1 now
where the time goes in v5:
time: 109 us
  Pallas kernels  107 us (98%)
  between operations  1.3 us (1%)
    pallas_call x3, Pallas kernels, call(): pl.pallas_call(kernel, out_shape=outs, in_specs=[vmem] * len(arrays), out...  91 us
    pallas_call x2, Pallas kernels, tile_product(): pl.pallas_call(functools.partial(product_kernel, transposed, out_blocks),...  14.5 us

profile of v5, /device:TPU:1, one launch (start us, length us, event | category | flops | bytes accessed | tf_op | source)
XLA Modules:
  0.0 108.6 jit_solution(9113160305005790972)
XLA Ops:
  1.3 20.5 %shard_map.111.source_ref = bf16[16,128,128]{2,1,0:T(8,128)(2,1)} custom-call(bf16[128,128]{1,0:T(8,128)(2,1)} %src.1), custom_call_target="tpu_custom_call" | custom-call | tf_op jit(solution)/shard_map/pallas_call | solution.py:386
  21.8 7.3 %shard_map.112.part = bf16[32,128,128]{2,1,0:T(8,128)(2,1)} custom-call(s32[128]{0:T(128)} %bitcast.10, s32[128]{0:T(128)} %bitcast.12, s32[1]{0:T(128)} %bitcast.6.count_ref, bf16[128,128,128]{2,1,0:T(8,128)(2,1)} %bitcast.8, bf16[16,128,128]{2,1,0:T(8,128)(2,1)} %shard_map.111.source_ref), custom_call_target="tpu_custom_call" | custom-call | tf_op jit(solution)/shard_map/pallas_call | solution.py:45
  29.1 46.9 %shard_map.113 = (f32[128,128]{1,0:T(8,128)}, bf16[32,128,128]{2,1,0:T(8,128)(2,1)}, f32[8,128]{1,0:T(8,128)}) custom-call(bf16[32,128,128]{2,1,0:T(8,128)(2,1)} %shard_map.112.part, f32[128,128]{1,0:T(8,128)} %weight.1, f32[1,128]{1,0:T(1,128)} %bitcast.14, bf16[128,128]{1,0:T(8,128)(2,1)} %cotangent.1), custom_call_target="tpu_custom_call" | custom-call | tf_op jit(solution)/shard_map/pallas_call | solution.py:386
  76.0 7.2 %shard_map.114.back = bf16[16,128,128]{2,1,0:T(8,128)(2,1)} custom-call(s32[128]{0:T(128)} %bitcast.13, s32[128]{0:T(128)} %bitcast.11, s32[1]{0:T(128)} %bitcast.7.count_ref, bf16[128,128,128]{2,1,0:T(8,128)(2,1)} %bitcast.9, bf16[32,128,128]{2,1,0:T(8,128)(2,1)} %get-tuple-element.14.source_ref), custom_call_target="tpu_custom_call" | custom-call | tf_op jit(solution)/shard_map/pallas_call | solution.py:45
  83.3 23.6 %shard_map.115 = (f32[128,128]{1,0:T(8,128)}, f32[32,8,128]{2,1,0:T(8,128)}) custom-call(bf16[16,128,128]{2,1,0:T(8,128)(2,1)} %shard_map.114.back, f32[8,128]{1,0:T(8,128)} %get-tuple-element.15.part), custom_call_target="tpu_custom_call" | custom-call | tf_op jit(solution)/shard_map/pallas_call | solution.py:386
  106.9 1.7 %shard_map.116 = (f32[128,128]{1,0:T(8,128)}, f32[128,128]{1,0:T(8,128)}, f32[128,128]{1,0:T(8,128)}, f32[1,128]{1,0:T(1,128)}) custom-call(f32[128,128]{1,0:T(8,128)} %get-tuple-element.13.hidden, f32[128,128]{1,0:T(8,128)} %get-tuple-element.16.grad_t, f32[32,8,128]{2,1,0:T(8,128)} %get-tuple-element.17.slices), custom_call_target="tpu_custom_call" | custom-call | tf_op jit(solution)/shard_map/pallas_call | solution.py:460
